TPU v7x, 32 devices: a whole 2x2x4 slice. The times are simulated.
32 devices in a mesh: tok: 4 (over z), feat: 8 (over y, x, core).
Axes of the slice: x: 2, y: 2, z: 4, core: 2. Of those that a mesh axis runs over, the one named last changes fastest.
Arguments:
- activations: bfloat16 [16384, 28672], P('tok', 'feat'), may hold values from -6 to 6
- out_grads: bfloat16 [16384, 8192], P('tok', 'feat'), may hold values from -6 to 6
- query_in: bfloat16 [8, 32, 28672], P('tok', None, 'feat'), may hold values from -0.03125 to 0.03125
- query_out: bfloat16 [8, 32, 8192], P('tok', None, 'feat'), may hold values from -0.0625 to 0.0625
Outputs:
- influence: float32 [8, 16384], P(None, ('tok', 'feat'))
All inputs are finite; a program needn't handle non-finite values.
Results may differ from a plain program's by a relative error of at most 0.0003.
Values may be sent and summed in bfloat16 or wider, within the bound.
A program may use at most 128 MiB of HBM per device.

v0:
```python
import jax
import jax.numpy as jnp
from jax import lax
from jax.sharding import PartitionSpec as P


def local(activations, out_grads, query_in, query_out):
    per_device, rank_size, in_local = query_in.shape
    row_count = activations.shape[0]
    factors = jnp.concatenate([query_in, query_out], axis=2)
    factor_block = lax.all_gather(factors, "tok", axis=0, tiled=True)
    pair_count = factor_block.shape[0] * rank_size
    in_side = factor_block[:, :, :in_local].reshape(pair_count, in_local)
    out_side = factor_block[:, :, in_local:].reshape(pair_count, -1)
    in_terms = lax.dot_general(
        activations, in_side, (((1,), (1,)), ((), ())), preferred_element_type=jnp.float32
    )
    out_terms = lax.dot_general(
        out_grads, out_side, (((1,), (1,)), ((), ())), preferred_element_type=jnp.float32
    )
    stacked = jnp.stack(
        [in_terms.reshape(row_count, -1, rank_size), out_terms.reshape(row_count, -1, rank_size)],
        axis=2,
    )
    terms = stacked.reshape(row_count, -1)
    summed = lax.psum_scatter(terms, "feat", scatter_dimension=0, tiled=True)
    grouped = summed.reshape(summed.shape[0], -1, 2, rank_size)
    return jnp.sum(grouped[:, :, 0, :] * grouped[:, :, 1, :], axis=2).T


def solution(mesh):
    in_specs = (P("tok", "feat"), P("tok", "feat"), P("tok", None, "feat"), P("tok", None, "feat"))
    out_specs = P(None, ("tok", "feat"))
    return jax.shard_map(local, mesh=mesh, in_specs=in_specs, out_specs=out_specs, check_vma=False)
```

profile of v0, /device:TPU:0, one launch (start us, length us, event | category | flops | bytes accessed | tf_op | source)
XLA Modules:
  0.0 165.7 jit_solution(5978298361538295682)
XLA Ops:
  6.5 0.0 all-gather.2.cloned.1.call-start
  6.5 1.9 %pad_maximum_fusion.1 = bf16[2,32,4608]{2,1,0:T(8,128)(2,1)} fusion(bf16[2,32,1024]{2,1,0:T(8,128)(2,1)} %param.7, bf16[2,32,3584]{2,1,0:T(8,128)(2,1)} %param.6), kind=kLoop, calls=%fused_computation.1 | loop fusion | flops 1179648 | bytes 1179648 | tf_op jit(solution)/shard_map/concatenate | solution.py:10
  8.5 0.0 all-gather.2.cloned.1.call-update
  8.5 0.0 reduce-scatter.2.cloned.1.call-start
  8.5 53.1 %all-gather.2.cloned.1.call-done = bf16[8,32,4608]{2,1,0:T(8,128)(2,1)} async-done(((bf16[2,32,4608]{2,1,0:T(8,128)(2,1)}), bf16[8,32,4608]{2,1,0:T(8,128)(2,1)}) %all-gather.2.cloned.1.call-update) | async-done | bytes 2359312 | tf_op jit(solution)/shard_map/all_gather | solution.py:11
  61.6 1.6 slice.16
  63.3 0.0 slice-start
  63.3 13.8 %fusion.1 = f32[256,4096]{1,0:T(8,128)S(1)} fusion(bf16[256,3584]{1,0:T(8,128)(2,1)S(1)} %bitcast.23, bf16[4096,3584]{1,0:T(8,128)(2,1)} %param.4), kind=kOutput, calls=%fused_computation.4 | convolution fusion | flops 7516192768 | bytes 35389440 | tf_op jit(solution)/shard_map/dot_general | solution.py:15
  77.1 0.0 slice-done
  77.1 5.7 %fusion.2 = f32[256,4096]{1,0:T(8,128)S(1)} fusion(bf16[256,1024]{1,0:T(8,128)(2,1)S(1)} %bitcast.22, bf16[4096,1024]{1,0:T(8,128)(2,1)} %param.5), kind=kOutput, calls=%fused_computation.5 | convolution fusion | flops 2147483648 | bytes 13107200 | tf_op jit(solution)/shard_map/dot_general | solution.py:18
  82.9 3.8 %pad_maximum_fusion = f32[4096,8,2,32]{0,3,2,1:T(8,128)} fusion(f32[4096,8,1,32]{0,3,2,1:T(8,128)S(1)} %bitcast.21, f32[4096,8,1,32]{0,3,2,1:T(8,128)S(1)} %bitcast.20), kind=kLoop, calls=%fused_computation | loop fusion | flops 2097152 | bytes 16777216 | tf_op jit(solution)/shard_map/stack | solution.py:21
  86.6 0.0 reduce-scatter.2.cloned.1.call-update
  86.7 70.2 %reduce-scatter.2.cloned.1.call-done = f32[512,512]{0,1:T(8,128)} async-done(((f32[4096,512]{0,1:T(8,128)}), f32[512,512]{0,1:T(8,128)}) %reduce-scatter.2.cloned.1.call-update) | async-done | bytes 1048592 | tf_op jit(solution)/shard_map/reduce_scatter | solution.py:26
  156.9 1.9 %fusion = f32[512,8]{0,1:T(8,128)} fusion(f32[512,8,2,32]{0,3,2,1:T(8,128)} %bitcast.24), kind=kLoop, calls=%fused_computation.3 | loop fusion | flops 258048 | bytes 1064960 | tf_op jit(solution)/shard_map/reduce_sum | solution.py:28
Async XLA Ops:
  6.5 55.1 %all-gather.2.cloned.1.call-start = ((), (), s32[]{:S(2)}) async-start(), calls=%async_computation.1 | async-start | bytes 2949120 | tf_op jit(solution)/shard_map/all_gather | solution.py:11
  8.5 148.4 %reduce-scatter.2.cloned.1.call-start = ((), (), s32[]{:S(2)}) async-start(), calls=%async_computation.2 | async-start | bytes 9437184 | tf_op jit(solution)/shard_map/reduce_scatter | solution.py:26
  63.3 13.8 %slice-start = ((bf16[8,32,4608]{2,1,0:T(8,128)(2,1)}), bf16[8,32,1024]{2,1,0:T(8,128)(2,1)S(1)}, s32[]{:S(2)}) async-start(bf16[8,32,4608]{2,1,0:T(8,128)(2,1)} %all-gather.2.cloned.1.call-done), calls=%async_computation.3 | async-start | bytes 1048576 | tf_op jit(solution)/shard_map/slice | solution.py:14
Sparse Core Ops, SparseCore 0:
  8.9 52.6 all-gather.1
  86.8 70.0 reduce-scatter.1
where the time goes:
time: 166 us
  waiting for transfers between devices  123 us (74%)
  matrix products  19.6 us (12%)
  between operations  13.4 us (8%)
  other arithmetic  7.63 us (5%)
    reduce_scatter x1, waiting for transfers between devices, local(): summed = lax.psum_scatter(terms, 'feat', scatter_dimension=0, tiled=True)  70.2 us
    all_gather x1, waiting for transfers between devices, local(): factor_block = lax.all_gather(factors, 'tok', axis=0, tiled=True)  53.1 us
    dot_general x1, matrix products, local(): lax.dot_general(activations, in_side, (((1,), (1,)), ((), ())), preferred...  13.8 us
    dot_general x1, matrix products, local(): lax.dot_general(out_grads, out_side, (((1,), (1,)), ((), ())), preferred_...  5.75 us
    another operation x1, other arithmetic, local(): jnp.stack([in_terms.reshape(row_count, -1, rank_size), out_terms.reshape(...  3.77 us
  transfers between devices with their start and end apart: 2, of which 2 were waited for; matrix products, arithmetic and copies ran while one was open for 0% of the time, Pallas kernels for 0%

commit v1 on v0

v1 whole, which is shorter than its diff:
```python
import functools

import jax
import jax.numpy as jnp
from jax import lax
from jax.experimental import pallas as pl
from jax.experimental.pallas import tpu as pltpu
from jax.sharding import PartitionSpec as P

MESH = pl.DeviceIdType.MESH
NT = (((1,), (1,)), ((), ()))


def kernel(
    n, nf, act, grad, qin, qout, out,
    a_buf, g_buf, fin, fout, acc, from_core, from_chip,
    a_sem, g_sem, own_sem, f_send, f_recv, core_send, core_recv, chip_send, chip_recv,
):
    me = lax.axis_index("tok")
    feat = lax.axis_index("feat")
    nc = nf // 2
    chip = feat // 2
    core = lax.rem(feat, 2)
    partner = chip * 2 + (1 - core)
    rows = acc.shape[2]
    cols = qin.shape[0]
    rank_queries = out.shape[0] // n
    rank = cols // rank_queries

    def peer_chip(shift):
        return lax.rem(chip + shift, nc) * 2

    def load(c, side):
        start = pl.multiple_of((peer_chip(nc - 1 - c) + side) * rows, rows)
        at = pl.ds(start, rows)
        slot = c + jnp.where(side == core, nc, 0)
        return (
            pltpu.make_async_copy(act.at[at], a_buf.at[at], a_sem.at[slot]),
            pltpu.make_async_copy(grad.at[at], g_buf.at[at], g_sem.at[slot]),
        )

    own_in = pltpu.make_async_copy(qin, fin.at[me, pl.ds(0, cols)], own_sem.at[0])
    own_out = pltpu.make_async_copy(qout, fout.at[me, pl.ds(cols, cols)], own_sem.at[1])
    own_in.start()
    own_out.start()
    for side in (1 - core, core):
        for c in range(nc):
            for copy in load(c, side):
                copy.start()

    for b in range(n):
        fin[b, cols:, :] = jnp.zeros((cols, fin.shape[2]), fin.dtype)
        fout[b, :cols, :] = jnp.zeros((cols, fout.shape[2]), fout.dtype)
    out[...] = jnp.zeros_like(out)

    barrier = pltpu.get_barrier_semaphore()
    pl.semaphore_signal(barrier, inc=1, device_id=(me, partner), device_id_type=MESH)
    for shift in range(1, nc):
        pl.semaphore_signal(
            barrier, inc=1, device_id=(me, peer_chip(shift) + core), device_id_type=MESH
        )

    @pl.when(me > 0)
    def _():
        pl.semaphore_signal(barrier, inc=1, device_id=(me - 1, feat), device_id_type=MESH)

    @pl.when(me < n - 1)
    def _():
        pl.semaphore_signal(barrier, inc=1, device_id=(me + 1, feat), device_id_type=MESH)

    beside = jnp.where(me > 0, 1, 0) + jnp.where(me < n - 1, 1, 0)
    pl.semaphore_wait(barrier, nc + beside)

    def pass_on(block, src_in, src_out, to, way):
        return (
            pltpu.make_async_remote_copy(
                src_ref=src_in, dst_ref=fin.at[block, pl.ds(0, cols)],
                send_sem=f_send.at[way, block, 0], recv_sem=f_recv.at[block, 0],
                device_id=(to, feat), device_id_type=MESH,
            ),
            pltpu.make_async_remote_copy(
                src_ref=src_out, dst_ref=fout.at[block, pl.ds(cols, cols)],
                send_sem=f_send.at[way, block, 1], recv_sem=f_recv.at[block, 1],
                device_id=(to, feat), device_id_type=MESH,
            ),
        )

    def forward(block, to, way):
        return pass_on(
            block, fin.at[block, pl.ds(0, cols)], fout.at[block, pl.ds(cols, cols)], to, way
        )

    @pl.when(me < n - 1)
    def _():
        for copy in pass_on(me, qin, qout, me + 1, 0):
            copy.start()

    @pl.when(me > 0)
    def _():
        for copy in pass_on(me, qin, qout, me - 1, 1):
            copy.start()

    inner = jnp.logical_and(me > 0, me < n - 1)

    def await_block(block):
        for copy in forward(block, lax.rem(me + 1, n), 0):
            copy.wait_recv()

    def arrive(d):
        @pl.when(jnp.logical_and(inner, me - d >= 0))
        def _():
            await_block(me - d)
            for copy in forward(me - d, me + 1, 0):
                copy.start()

        @pl.when(jnp.logical_and(inner, me + d <= n - 1))
        def _():
            await_block(me + d)
            for copy in forward(me + d, me - 1, 1):
                copy.start()

    near = jnp.minimum(me, n - 1 - me)
    long_left = me > n - 1 - me

    def block_of(i):
        paired = (i + 1) // 2
        far = i - near
        both = jnp.where(lax.rem(i, 2) == 1, me - paired, me + paired)
        one = jnp.where(long_left, me - far, me + far)
        return jnp.where(i == 0, me, jnp.where(i <= 2 * near, both, one))

    def to_core(i, c):
        return pltpu.make_async_remote_copy(
            src_ref=acc.at[i, c], dst_ref=from_core.at[i, c],
            send_sem=core_send.at[i, c], recv_sem=core_recv.at[i, c],
            device_id=(me, partner), device_id_type=MESH,
        )

    def to_chip(i, c):
        return pltpu.make_async_remote_copy(
            src_ref=acc.at[i, nc + c], dst_ref=from_chip.at[i, c],
            send_sem=chip_send.at[i, c], recv_sem=chip_recv.at[i, c],
            device_id=(me, peer_chip(nc - 1 - c) + core), device_id_type=MESH,
        )

    def project(block, c, side):
        start = pl.multiple_of((peer_chip(nc - 1 - c) + side) * rows, rows)
        at = pl.ds(start, rows)
        return lax.dot_general(
            a_buf[at, :], fin[block], NT, preferred_element_type=jnp.float32
        ) + lax.dot_general(
            g_buf[at, :], fout[block], NT, preferred_element_type=jnp.float32
        )

    def finish(i):
        block = block_of(i)
        total = acc[i, 2 * nc - 1]
        for c in range(nc - 1):
            to_chip(i, c).wait_recv()
            total = total + from_chip[i, c]
        product = total * pltpu.roll(total, cols, 1)
        lane = lax.broadcasted_iota(jnp.int32, (out.shape[0], 2 * cols), 1)
        row = lax.broadcasted_iota(jnp.int32, (out.shape[0], 2 * cols), 0)
        first = (row - block * rank_queries) * rank
        mine = (lane >= first) & (lane < first + rank) & (lane < cols)
        chosen = jnp.where(mine, 1.0, 0.0).astype(jnp.float32)
        out[...] += lax.dot_general(
            chosen, product, NT, preferred_element_type=jnp.float32,
            precision=lax.Precision.HIGHEST,
        )

    def slot(i, carry):
        block = block_of(i)

        @pl.when(i == 0)
        def _():
            own_in.wait()
            own_out.wait()

        @pl.when(jnp.logical_and(i > 0, jnp.logical_not(inner)))
        def _():
            await_block(block)

        @pl.when(i == 1)
        def _():
            arrive(1)

        def theirs(c, carry):
            @pl.when(i == 0)
            def _():
                for copy in load(c, 1 - core):
                    copy.wait()

            acc[i, c] = project(block, c, 1 - core)
            to_core(i, c).start()
            return carry

        lax.fori_loop(0, nc, theirs, 0)

        @pl.when(i > 0)
        def _():
            finish(i - 1)

        @pl.when(jnp.logical_and(i >= 2, i <= n - 2))
        def _():
            arrive(i)

        def ours(c, carry):
            @pl.when(i == 0)
            def _():
                for copy in load(c, core):
                    copy.wait()

            mine = project(block, c, core)
            to_core(i, c).wait_recv()
            acc[i, nc + c] = mine + from_core[i, c]

            @pl.when(c < nc - 1)
            def _():
                to_chip(i, c).start()

            return carry

        lax.fori_loop(0, nc, ours, 0)
        return carry

    lax.fori_loop(0, n, slot, 0)
    finish(n - 1)

    def drain(i, carry):
        def cores(c, carry):
            to_core(i, c).wait_send()
            return carry

        def chips(c, carry):
            to_chip(i, c).wait_send()
            return carry

        lax.fori_loop(0, nc, cores, 0)
        lax.fori_loop(0, nc - 1, chips, 0)
        return carry

    lax.fori_loop(0, n, drain, 0)

    def drain_blocks(b, carry):
        @pl.when(jnp.logical_and(me < n - 1, b <= me))
        def _():
            for copy in forward(b, lax.rem(me + 1, n), 0):
                copy.wait_send()

        @pl.when(jnp.logical_and(me > 0, b >= me))
        def _():
            for copy in forward(b, lax.rem(me + 1, n), 1):
                copy.wait_send()

        return carry

    lax.fori_loop(0, n, drain_blocks, 0)


def local(n, nf, activations, out_grads, query_in, query_out):
    per_device, rank, in_local = query_in.shape
    out_local = query_out.shape[2]
    cols = per_device * rank
    tokens = activations.shape[0]
    rows = tokens // nf
    nc = nf // 2
    dma = pltpu.SemaphoreType.DMA
    any_space = pl.BlockSpec(memory_space=pl.ANY)
    return pl.pallas_call(
        functools.partial(kernel, n, nf),
        out_shape=jax.ShapeDtypeStruct((n * per_device, rows), jnp.float32),
        in_specs=[any_space] * 4,
        out_specs=pl.BlockSpec(memory_space=pltpu.VMEM),
        scratch_shapes=[
            pltpu.VMEM((tokens, in_local), activations.dtype),
            pltpu.VMEM((tokens, out_local), out_grads.dtype),
            pltpu.VMEM((n, 2 * cols, in_local), query_in.dtype),
            pltpu.VMEM((n, 2 * cols, out_local), query_out.dtype),
            pltpu.VMEM((n, nf, rows, 2 * cols), jnp.float32),
            pltpu.VMEM((n, nc, rows, 2 * cols), jnp.float32),
            pltpu.VMEM((n, nc - 1, rows, 2 * cols), jnp.float32),
            dma((nf,)),
            dma((nf,)),
            dma((2,)),
            dma((2, n, 2)),
            dma((n, 2)),
            dma((n, nc)),
            dma((n, nc)),
            dma((n, nc - 1)),
            dma((n, nc - 1)),
        ],
        compiler_params=pltpu.CompilerParams(
            collective_id=0, has_side_effects=True, vmem_limit_bytes=66_000_000
        ),
    )(
        activations, out_grads,
        query_in.reshape(cols, in_local), query_out.reshape(cols, out_local),
    )


def solution(mesh):
    n, nf = mesh.shape["tok"], mesh.shape["feat"]
    in_specs = (P("tok", "feat"), P("tok", "feat"), P("tok", None, "feat"), P("tok", None, "feat"))
    out_specs = P(None, ("tok", "feat"))
    return jax.shard_map(
        functools.partial(local, n, nf),
        mesh=mesh, in_specs=in_specs, out_specs=out_specs, check_vma=False,
    )
```

time: 166 us -> 87.5 us (0.53)
  waiting for transfers between devices: 123 us -> 0 us
  Pallas kernels: 0 us -> 85.9 us
  matrix products: 19.6 us -> 0 us
  between operations: 13.4 us -> 0.01 us
  other arithmetic: 7.63 us -> 0 us
    pallas_call x0 -> x1, Pallas kernels: none -> 85.9 us  [local(): pl.pallas_call(functools.partial(kernel, n, nf), out_shape=jax.ShapeDtype...]
    reduce_scatter x1 -> x0, waiting for transfers between devices: 70.2 us -> none  [local(): summed = lax.psum_scatter(terms, 'feat', scatter_dimension=0, tiled=True)]
    all_gather x1 -> x0, waiting for transfers between devices: 53.1 us -> none  [local(): factor_block = lax.all_gather(factors, 'tok', axis=0, tiled=True)]
    dot_general x2 -> x0, matrix products: 19.6 us -> none  [the longest x1 13.8 us: local(): lax.dot_general(activations, in_side, (((1,), (1,)), ((), ())), preferred...]
    another operation x1 -> x0, other arithmetic: 3.77 us -> none  [local(): jnp.stack([in_terms.reshape(row_count, -1, rank_size), out_terms.reshape(...]
    concatenate x1 -> x0, other arithmetic: 1.94 us -> none  [local(): factors = jnp.concatenate([query_in, query_out], axis=2)]
    reduce_sum x1 -> x0, other arithmetic: 1.92 us -> none  [local(): return jnp.sum(grouped[:, :, 0, :] * grouped[:, :, 1, :], axis=2).T]
  transfers between devices with their start and end apart: 2 -> 0, of which waited for: 2 -> 0; matrix products, arithmetic and copies ran while one was open for 0% -> 0% of each run, Pallas kernels for 0% -> 0%
where the time goes in v1:
time: 87.5 us; the launch traced here: 87.2 us
  Pallas kernels  85.9 us (98%)
  local copies, waits for them, and re-layouts  1.32 us (2%)
    pallas_call x1, Pallas kernels, local(): pl.pallas_call(functools.partial(kernel, n, nf), out_shape=jax.ShapeDtype...  85.9 us

profile of v1, /device:TPU:0, one launch (start us, length us, event | category | flops | bytes accessed | tf_op | source)
XLA Modules:
  0.0 87.2 jit_solution(7298720106465390100)
XLA Ops:
  0.0 85.9 %shard_map.46 = f32[8,512]{1,0:T(8,128)} custom-call(bf16[4096,3584]{1,0:T(8,128)(2,1)} %act.1, bf16[4096,1024]{1,0:T(8,128)(2,1)} %grad.1, bf16[64,3584]{1,0:T(8,128)(2,1)} %bitcast.2, bf16[64,1024]{1,0:T(8,128)(2,1)} %bitcast.3), custom_call_target="tpu_custom_call" | custom-call | tf_op jit(solution)/shard_map/pallas_call | solution.py:270
  85.9 1.3 %copy.6 = f32[8,512]{1,0:T(8,128)} copy(f32[8,512]{1,0:T(8,128)} %shard_map.46) | data formatting | bytes 32768

commit v2 on v1

--- a/solution.py
+++ b/solution.py
@@ -8,13 +8,15 @@
 from jax.sharding import PartitionSpec as P
 
 MESH = pl.DeviceIdType.MESH
+RELAY = 1
 NT = (((1,), (1,)), ((), ()))
 
 
 def kernel(
     n, nf, act, grad, qin, qout, out,
-    a_buf, g_buf, fin, fout, acc, from_core, from_chip,
-    a_sem, g_sem, own_sem, f_send, f_recv, core_send, core_recv, chip_send, chip_recv,
+    a_buf, g_buf, fin, fout, acc, from_core, x_first, y_first, y_last, x_last,
+    a_sem, g_sem, own_sem, f_send, f_recv, core_send, core_recv,
+    xf_send, xf_recv, yf_send, yf_recv, yl_send, yl_recv, xl_send, xl_recv,
 ):
     me = lax.axis_index("tok")
     feat = lax.axis_index("feat")
@@ -27,11 +29,18 @@
     rank_queries = out.shape[0] // n
     rank = cols // rank_queries
 
-    def peer_chip(shift):
-        return lax.rem(chip + shift, nc) * 2
+    ny = nc // 2
+    half = rows // 2
+    x, y = lax.rem(chip, 2), chip // 2
+
+    def peer(dy, dx):
+        return (lax.rem(y + dy, ny) * 2 + lax.rem(x + dx, 2)) * 2
+
+    def peer_at(c):
+        return peer(lax.rem(ny - 1 - lax.rem(c, ny) + ny, ny), jnp.where(c < ny, 1, 0))
 
     def load(c, side):
-        start = pl.multiple_of((peer_chip(nc - 1 - c) + side) * rows, rows)
+        start = pl.multiple_of((peer_at(c) + side) * rows, rows)
         at = pl.ds(start, rows)
         slot = c + jnp.where(side == core, nc, 0)
         return (
@@ -55,10 +64,11 @@
 
     barrier = pltpu.get_barrier_semaphore()
     pl.semaphore_signal(barrier, inc=1, device_id=(me, partner), device_id_type=MESH)
-    for shift in range(1, nc):
+    for dy in range(1, ny):
         pl.semaphore_signal(
-            barrier, inc=1, device_id=(me, peer_chip(shift) + core), device_id_type=MESH
-        )
+            barrier, inc=1, device_id=(me, peer(dy, 0) + core), device_id_type=MESH
+        )
+    pl.semaphore_signal(barrier, inc=1, device_id=(me, peer(0, 1) + core), device_id_type=MESH)
 
     @pl.when(me > 0)
     def _():
@@ -69,7 +79,7 @@
         pl.semaphore_signal(barrier, inc=1, device_id=(me + 1, feat), device_id_type=MESH)
 
     beside = jnp.where(me > 0, 1, 0) + jnp.where(me < n - 1, 1, 0)
-    pl.semaphore_wait(barrier, nc + beside)
+    pl.semaphore_wait(barrier, ny + 1 + beside)
 
     def pass_on(block, src_in, src_out, to, way):
         return (
@@ -136,15 +146,51 @@
             device_id=(me, partner), device_id_type=MESH,
         )
 
-    def to_chip(i, c):
+    top, low = pl.ds(0, half), pl.ds(half, half)
+
+    def send(src, dst, send_sem, recv_sem, dy, dx):
         return pltpu.make_async_remote_copy(
-            src_ref=acc.at[i, nc + c], dst_ref=from_chip.at[i, c],
-            send_sem=chip_send.at[i, c], recv_sem=chip_recv.at[i, c],
-            device_id=(me, peer_chip(nc - 1 - c) + core), device_id_type=MESH,
-        )
+            src_ref=src, dst_ref=dst, send_sem=send_sem, recv_sem=recv_sem,
+            device_id=(me, peer(dy, dx) + core), device_id_type=MESH,
+        )
+
+    def along_x(i, dy):
+        return send(
+            acc.at[i, nc + ny - 1 - dy, top], x_first.at[i, dy],
+            xf_send.at[i, dy], xf_recv.at[i, dy], 0, 1,
+        )
+
+    def along_y(i, dy, dx):
+        return send(
+            acc.at[i, 2 * nc - 1 - dx * ny - dy, low], y_first.at[i, dy - 1, dx],
+            yf_send.at[i, dy - 1, dx], yf_recv.at[i, dy - 1, dx], dy, 0,
+        )
+
+    def then_y(i, dy):
+        return send(
+            acc.at[i, 2 * nc - 1 - dy, top], y_last.at[i, dy - 1],
+            yl_send.at[i, dy - 1], yl_recv.at[i, dy - 1], dy, 0,
+        )
+
+    def then_x(i):
+        return send(
+            acc.at[i, nc + ny - 1, low], x_last.at[i], xl_send.at[i], xl_recv.at[i], 0, 1
+        )
+
+    def relay(i):
+        for dy in range(ny - 1, 0, -1):
+            along_x(i, dy).wait_recv()
+            acc[i, 2 * nc - 1 - dy, :half, :] += x_first[i, dy]
+            then_y(i, dy).start()
+        total = acc[i, nc + ny - 1, half:, :]
+        for dy in range(ny - 1, 0, -1):
+            along_y(i, dy, 1).wait_recv()
+            total = total + y_first[i, dy - 1, 1]
+        acc[i, nc + ny - 1, half:, :] = total
+        then_x(i).start()
 
     def project(block, c, side):
-        start = pl.multiple_of((peer_chip(nc - 1 - c) + side) * rows, rows)
+        start = pl.multiple_of((peer_at(c) + side) * rows, rows)
         at = pl.ds(start, rows)
         return lax.dot_general(
             a_buf[at, :], fin[block], NT, preferred_element_type=jnp.float32
@@ -154,10 +200,18 @@
 
     def finish(i):
         block = block_of(i)
-        total = acc[i, 2 * nc - 1]
-        for c in range(nc - 1):
-            to_chip(i, c).wait_recv()
-            total = total + from_chip[i, c]
+        along_x(i, 0).wait_recv()
+        upper = acc[i, 2 * nc - 1, :half, :] + x_first[i, 0]
+        lower = acc[i, 2 * nc - 1, half:, :]
+        for dy in range(ny - 1, 0, -1):
+            along_y(i, dy, 0).wait_recv()
+            lower = lower + y_first[i, dy - 1, 0]
+        for dy in range(ny - 1, 0, -1):
+            then_y(i, dy).wait_recv()
+            upper = upper + y_last[i, dy - 1]
+        then_x(i).wait_recv()
+        lower = lower + x_last[i]
+        total = jnp.concatenate([upper, lower], axis=0)
         product = total * pltpu.roll(total, cols, 1)
         lane = lax.broadcasted_iota(jnp.int32, (out.shape[0], 2 * cols), 1)
         row = lax.broadcasted_iota(jnp.int32, (out.shape[0], 2 * cols), 0)
@@ -197,9 +251,9 @@
 
         lax.fori_loop(0, nc, theirs, 0)
 
-        @pl.when(i > 0)
-        def _():
-            finish(i - 1)
+        @pl.when(i > 1)
+        def _():
+            finish(i - 2)
 
         @pl.when(jnp.logical_and(i >= 2, i <= n - 2))
         def _():
@@ -215,9 +269,19 @@
             to_core(i, c).wait_recv()
             acc[i, nc + c] = mine + from_core[i, c]
 
-            @pl.when(c < nc - 1)
+            for k in range(nc - 1):
+                dx, dy = 1 - k // ny, ny - 1 - k % ny
+
+                @pl.when(c == k)
+                def _():
+                    if dx:
+                        along_x(i, dy).start()
+                    if dy:
+                        along_y(i, dy, dx).start()
+
+            @pl.when(jnp.logical_and(i > 0, c == RELAY))
             def _():
-                to_chip(i, c).start()
+                relay(i - 1)
 
             return carry
 
@@ -225,6 +289,8 @@
         return carry
 
     lax.fori_loop(0, n, slot, 0)
+    finish(n - 2)
+    relay(n - 1)
     finish(n - 1)
 
     def drain(i, carry):
@@ -232,12 +298,15 @@
             to_core(i, c).wait_send()
             return carry
 
-        def chips(c, carry):
-            to_chip(i, c).wait_send()
-            return carry
+        for dy in range(ny):
+            along_x(i, dy).wait_send()
+        for dy in range(1, ny):
+            along_y(i, dy, 0).wait_send()
+            along_y(i, dy, 1).wait_send()
+            then_y(i, dy).wait_send()
+        then_x(i).wait_send()
 
         lax.fori_loop(0, nc, cores, 0)
-        lax.fori_loop(0, nc - 1, chips, 0)
         return carry
 
     lax.fori_loop(0, n, drain, 0)
@@ -265,6 +334,7 @@
     tokens = activations.shape[0]
     rows = tokens // nf
     nc = nf // 2
+    ny = nc // 2
     dma = pltpu.SemaphoreType.DMA
     any_space = pl.BlockSpec(memory_space=pl.ANY)
     return pl.pallas_call(
@@ -279,7 +349,10 @@
             pltpu.VMEM((n, 2 * cols, out_local), query_out.dtype),
             pltpu.VMEM((n, nf, rows, 2 * cols), jnp.float32),
             pltpu.VMEM((n, nc, rows, 2 * cols), jnp.float32),
-            pltpu.VMEM((n, nc - 1, rows, 2 * cols), jnp.float32),
+            pltpu.VMEM((n, ny, rows // 2, 2 * cols), jnp.float32),
+            pltpu.VMEM((n, ny - 1, 2, rows // 2, 2 * cols), jnp.float32),
+            pltpu.VMEM((n, ny - 1, rows // 2, 2 * cols), jnp.float32),
+            pltpu.VMEM((n, rows // 2, 2 * cols), jnp.float32),
             dma((nf,)),
             dma((nf,)),
             dma((2,)),
@@ -287,8 +360,14 @@
             dma((n, 2)),
             dma((n, nc)),
             dma((n, nc)),
-            dma((n, nc - 1)),
-            dma((n, nc - 1)),
+            dma((n, ny)),
+            dma((n, ny)),
+            dma((n, ny - 1, 2)),
+            dma((n, ny - 1, 2)),
+            dma((n, ny - 1)),
+            dma((n, ny - 1)),
+            dma((n,)),
+            dma((n,)),
         ],
         compiler_params=pltpu.CompilerParams(
             collective_id=0, has_side_effects=True, vmem_limit_bytes=66_000_000

time: 87.5 us -> 82 us (0.937)
  Pallas kernels: 85.9 us -> 80.4 us
    pallas_call x1, Pallas kernels: 85.9 us -> 80.4 us  [local(): pl.pallas_call(functools.partial(kernel, n, nf), out_shape=jax.ShapeDtype...]
where the time goes in v2:
time: 82 us; the launch traced here: 81.7 us
  Pallas kernels  80.4 us (98%)
  local copies, waits for them, and re-layouts  1.32 us (2%)
    pallas_call x1, Pallas kernels, local(): pl.pallas_call(functools.partial(kernel, n, nf), out_shape=jax.ShapeDtype...  80.4 us

profile of v2, /device:TPU:0, one launch (start us, length us, event | category | flops | bytes accessed | tf_op | source)
XLA Modules:
  0.0 81.7 jit_solution(15375158456355484970)
XLA Ops:
  0.0 80.4 %shard_map.46 = f32[8,512]{1,0:T(8,128)} custom-call(bf16[4096,3584]{1,0:T(8,128)(2,1)} %act.1, bf16[4096,1024]{1,0:T(8,128)(2,1)} %grad.1, bf16[64,3584]{1,0:T(8,128)(2,1)} %bitcast.2, bf16[64,1024]{1,0:T(8,128)(2,1)} %bitcast.3), custom_call_target="tpu_custom_call" | custom-call | tf_op jit(solution)/shard_map/pallas_call | solution.py:340
  80.4 1.3 %copy.6 = f32[8,512]{1,0:T(8,128)} copy(f32[8,512]{1,0:T(8,128)} %shard_map.46) | data formatting | bytes 32768

commit v3 on v2

--- a/solution.py
+++ b/solution.py
@@ -9,6 +9,7 @@
 
 MESH = pl.DeviceIdType.MESH
 RELAY = 1
+PASS_ON = 2
 NT = (((1,), (1,)), ((), ()))
 
 
@@ -48,8 +49,8 @@
             pltpu.make_async_copy(grad.at[at], g_buf.at[at], g_sem.at[slot]),
         )
 
-    own_in = pltpu.make_async_copy(qin, fin.at[me, pl.ds(0, cols)], own_sem.at[0])
-    own_out = pltpu.make_async_copy(qout, fout.at[me, pl.ds(cols, cols)], own_sem.at[1])
+    own_in = pltpu.make_async_copy(qin, fin.at[me], own_sem.at[0])
+    own_out = pltpu.make_async_copy(qout, fout.at[me], own_sem.at[1])
     own_in.start()
     own_out.start()
     for side in (1 - core, core):
@@ -57,9 +58,6 @@
             for copy in load(c, side):
                 copy.start()
 
-    for b in range(n):
-        fin[b, cols:, :] = jnp.zeros((cols, fin.shape[2]), fin.dtype)
-        fout[b, :cols, :] = jnp.zeros((cols, fout.shape[2]), fout.dtype)
     out[...] = jnp.zeros_like(out)
 
     barrier = pltpu.get_barrier_semaphore()
@@ -84,12 +82,12 @@
     def pass_on(block, src_in, src_out, to, way):
         return (
             pltpu.make_async_remote_copy(
-                src_ref=src_in, dst_ref=fin.at[block, pl.ds(0, cols)],
+                src_ref=src_in, dst_ref=fin.at[block],
                 send_sem=f_send.at[way, block, 0], recv_sem=f_recv.at[block, 0],
                 device_id=(to, feat), device_id_type=MESH,
             ),
             pltpu.make_async_remote_copy(
-                src_ref=src_out, dst_ref=fout.at[block, pl.ds(cols, cols)],
+                src_ref=src_out, dst_ref=fout.at[block],
                 send_sem=f_send.at[way, block, 1], recv_sem=f_recv.at[block, 1],
                 device_id=(to, feat), device_id_type=MESH,
             ),
@@ -97,7 +95,7 @@
 
     def forward(block, to, way):
         return pass_on(
-            block, fin.at[block, pl.ds(0, cols)], fout.at[block, pl.ds(cols, cols)], to, way
+            block, fin.at[block], fout.at[block], to, way
         )
 
     @pl.when(me < n - 1)
@@ -192,11 +190,13 @@
     def project(block, c, side):
         start = pl.multiple_of((peer_at(c) + side) * rows, rows)
         at = pl.ds(start, rows)
-        return lax.dot_general(
+        in_side = lax.dot_general(
             a_buf[at, :], fin[block], NT, preferred_element_type=jnp.float32
-        ) + lax.dot_general(
+        )
+        out_side = lax.dot_general(
             g_buf[at, :], fout[block], NT, preferred_element_type=jnp.float32
         )
+        return jnp.concatenate([in_side, out_side], axis=1)
 
     def finish(i):
         block = block_of(i)
@@ -235,10 +235,6 @@
         def _():
             await_block(block)
 
-        @pl.when(i == 1)
-        def _():
-            arrive(1)
-
         def theirs(c, carry):
             @pl.when(i == 0)
             def _():
@@ -255,15 +251,15 @@
         def _():
             finish(i - 2)
 
-        @pl.when(jnp.logical_and(i >= 2, i <= n - 2))
-        def _():
-            arrive(i)
-
         def ours(c, carry):
             @pl.when(i == 0)
             def _():
                 for copy in load(c, core):
                     copy.wait()
+
+            @pl.when(jnp.logical_and(i < n - 2, c == PASS_ON))
+            def _():
+                arrive(i + 1)
 
             mine = project(block, c, core)
             to_core(i, c).wait_recv()
@@ -289,8 +285,8 @@
         return carry
 
     lax.fori_loop(0, n, slot, 0)
+    relay(n - 1)
     finish(n - 2)
-    relay(n - 1)
     finish(n - 1)
 
     def drain(i, carry):
@@ -345,8 +341,8 @@
         scratch_shapes=[
             pltpu.VMEM((tokens, in_local), activations.dtype),
             pltpu.VMEM((tokens, out_local), out_grads.dtype),
-            pltpu.VMEM((n, 2 * cols, in_local), query_in.dtype),
-            pltpu.VMEM((n, 2 * cols, out_local), query_out.dtype),
+            pltpu.VMEM((n, cols, in_local), query_in.dtype),
+            pltpu.VMEM((n, cols, out_local), query_out.dtype),
             pltpu.VMEM((n, nf, rows, 2 * cols), jnp.float32),
             pltpu.VMEM((n, nc, rows, 2 * cols), jnp.float32),
             pltpu.VMEM((n, ny, rows // 2, 2 * cols), jnp.float32),

time: 82 us -> 74.9 us (0.913)
  Pallas kernels: 80.4 us -> 73.3 us
    pallas_call x1, Pallas kernels: 80.4 us -> 73.3 us  [local(): pl.pallas_call(functools.partial(kernel, n, nf), out_shape=jax.ShapeDtype...]
where the time goes in v3:
time: 74.9 us; the launch traced here: 74.7 us
  Pallas kernels  73.3 us (98%)
  local copies, waits for them, and re-layouts  1.32 us (2%)
    pallas_call x1, Pallas kernels, local(): pl.pallas_call(functools.partial(kernel, n, nf), out_shape=jax.ShapeDtype...  73.3 us

profile of v3, /device:TPU:0, one launch (start us, length us, event | category | flops | bytes accessed | tf_op | source)
XLA Modules:
  0.0 74.7 jit_solution(11514551222836573119)
XLA Ops:
  0.0 73.3 %shard_map.46 = f32[8,512]{1,0:T(8,128)} custom-call(bf16[4096,3584]{1,0:T(8,128)(2,1)} %act.1, bf16[4096,1024]{1,0:T(8,128)(2,1)} %grad.1, bf16[64,3584]{1,0:T(8,128)(2,1)} %bitcast.2, bf16[64,1024]{1,0:T(8,128)(2,1)} %bitcast.3), custom_call_target="tpu_custom_call" | custom-call | tf_op jit(solution)/shard_map/pallas_call | solution.py:336
  73.3 1.3 %copy.6 = f32[8,512]{1,0:T(8,128)} copy(f32[8,512]{1,0:T(8,128)} %shard_map.46) | data formatting | bytes 32768
